TPU v7x, 256 devices: a whole 4x4x8 slice. The times are simulated.
256 devices in a mesh: rows: 64 (over z_lo, y, x, core), cols: 4 (over z_hi).
Axes of the slice: x: 4, y: 4, z: 8 (z_hi: 4, z_lo: 2; z = z_hi * 2 + z_lo), core: 2. Of those that a mesh axis runs over, the one named last changes fastest.
Arguments:
- design: bfloat16 [256, 1048576], P(None, 'rows'), may hold values from -0.28125 to 0.28125
- targets: bfloat16 [128, 1048576], P('cols', 'rows'), may hold values from -8 to 8
- flip_bits: int32 [2, 1048576], P(None, 'rows'), may hold values from 0 to 1
- listed: int32 [2, 32768], P(None, 'rows'), may hold values from 0 to 16383
- block_order: int32 [2, 64, 16], P(None, 'rows'), may hold values from 0 to 15, each once within a row
Outputs:
- solution: float32 [256, 128], P(None, 'cols')
- residual: float32 [128, 1048576], P('cols', 'rows')
Inputs may be any that keep to these rules, and one draw needn't show every extreme that they name: A group's listed rows are its own rows, counted from its first row; repeats may occur. `block_order`: for each step and group the 16 entries are a permutation.
All inputs are finite; a program needn't handle non-finite values.
Results may differ from a plain program's by a relative error of at most 0.017.
Values sent between devices are 32-bit elements; how exact they have to be, the bound alone decides.
A program may use at most 64 MiB of HBM per device.

v0:
```python
import math
import jax
import jax.numpy as jnp
from jax import lax
from jax.sharding import PartitionSpec as P


def on_device(design, targets, flip_bits, listed, block_order):
    unknowns, rows_here = design.shape
    steps_count = flip_bits.shape[0]
    blocks_count = block_order.shape[2]
    block_len = rows_here // blocks_count
    pick_count = listed.shape[1]
    col_share = unknowns // lax.axis_size("cols")
    inv_root = 1.0 / math.sqrt(block_len)
    keep_scale = math.sqrt(rows_here / pick_count)
    own_rows = lax.dynamic_slice_in_dim(design, lax.axis_index("cols") * col_share, col_share, 0)
    positions = jnp.arange(block_len, dtype=jnp.int32)[:, None]
    block_ids = jnp.arange(blocks_count, dtype=jnp.int32)[:, None]
    unit_eye = jnp.eye(unknowns, dtype=jnp.float32)

    def misfit_of(solution):
        product = lax.dot_general(
            solution.astype(jnp.bfloat16),
            design,
            (((0,), (0,)), ((), ())),
            preferred_element_type=jnp.float32,
        )
        return product - targets.astype(jnp.float32)

    solution = jnp.zeros((unknowns, targets.shape[0]), jnp.float32)
    for step_index in range(steps_count):
        sign_rows = (
            (2 * flip_bits[step_index] - 1).astype(jnp.bfloat16).reshape(blocks_count, block_len)
        )
        chosen = listed[step_index]
        order_now = block_order[step_index, 0]
        target_block = chosen // block_len
        within = chosen % block_len
        source = jnp.sum(
            jnp.where(target_block[None, :] == block_ids, order_now[:, None], 0), axis=0
        )
        parity = jnp.zeros((block_len, pick_count), jnp.int32)
        for bit_index in range(block_len.bit_length() - 1):
            parity = parity ^ positions >> bit_index & 1 & (within[None, :] >> bit_index & 1)
        walsh = (1 - 2 * parity).astype(jnp.bfloat16)
        placed = (source[None, :] == block_ids).astype(jnp.bfloat16)
        table = (placed[:, None, :] * sign_rows[:, :, None] * walsh[None, :, :]).reshape(
            rows_here, pick_count
        )
        mixed_rows = (
            jnp.dot(own_rows, table, preferred_element_type=jnp.float32) * inv_root
        ).astype(jnp.bfloat16)
        summed = lax.psum((mixed_rows.astype(jnp.float32) * keep_scale)[None], "rows")
        whole_sketch = lax.all_gather(summed, "cols", axis=1, tiled=True)
        gram_stack = jnp.einsum(
            "npm,nqm->npq", whole_sketch, whole_sketch, precision=lax.Precision.HIGHEST
        )
        shift = jnp.trace(gram_stack, axis1=1, axis2=2) / unknowns
        gram_now = (gram_stack + shift[:, None, None] * unit_eye[None])[0]
        if step_index == 0:
            misfit_half = -targets
        else:
            misfit_half = misfit_of(solution).astype(jnp.bfloat16)
        local_grad = lax.dot_general(
            design, misfit_half, (((1,), (1,)), ((), ())), preferred_element_type=jnp.float32
        )
        gradient = lax.psum(local_grad, "rows")
        factor = jnp.linalg.cholesky(gram_now)
        solution = solution - jax.scipy.linalg.cho_solve((factor, True), gradient)
    return (solution, misfit_of(solution))


def solution(mesh):
    return jax.shard_map(
        on_device,
        mesh=mesh,
        in_specs=(
            P(None, "rows"),
            P("cols", "rows"),
            P(None, "rows"),
            P(None, "rows"),
            P(None, "rows", None),
        ),
        out_specs=(P(None, "cols"), P("cols", "rows")),
        check_vma=False,
    )
```

profile of v0, /device:TPU:32, one launch (start us, length us, event | category | flops | bytes accessed | tf_op | source)
XLA Modules:
  0.0 1007.5 jit_solution(7467058959739676185)
XLA Ops:
  7.3 0.8 and_select_fusion.3
  8.1 0.7 slice_bitcast_fusion.13
  8.9 1.4 convert_reduce_fusion.1
  10.4 2.0 subtract_convert_fusion.1
  12.4 2.8 bitcast_multiply_fusion.2
  15.2 3.7 fusion.32
  18.9 2.0 subtract_convert_fusion
  20.9 2.8 bitcast_multiply_fusion
  23.7 3.7 fusion.20
  27.4 6.0 fusion.35
  33.4 279.1 %psum.29 = f32[256,32]{0,1:T(8,128)S(1)} all-reduce(f32[256,32]{0,1:T(8,128)S(1)} %fusion.35), channel_id=1, replica_groups=mesh['rows'=64,'cols'=4] {'rows'}, use_global_device_ids=true, to_apply=%region_7.9 | all-reduce | flops 8192 | bytes 65536 | tf_op jit(solution)/shard_map/psum | solution.py:68
  312.5 231.7 %all-reduce.4.cloned.1.call-done = (f32[1,64,512]{2,1,0:T(8,128)}, f32[1,64,512]{2,1,0:T(8,128)}) async-done(((f32[1,64,512]{2,1,0:T(8,128)}, f32[1,64,512]{2,1,0:T(8,128)}), (f32[1,64,512]{2,1,0:T(8,128)}, f32[1,64,512]{2,1,0:T(8,128)})) %all-reduce.4.cloned.1.call-update) | async-done | bytes 262160 | tf_op jit(solution)/shard_map/psum | solution.py:54
  544.2 18.6 %all_gather.6 = f32[1,256,512]{2,1,0:T(8,128)S(1)} all-gather(f32[1,64,512]{2,1,0:T(8,128)} %get-tuple-element.39), channel_id=1, replica_groups=mesh['rows'=64,'cols'=4] {'cols'}, dimensions={1}, use_global_device_ids=true | all-gather | bytes 655360 | tf_op jit(solution)/shard_map/all_gather | solution.py:55
  562.8 1.2 select_reduce_fusion.1
  564.9 11.7 %cholesky.130 = f32[128,128]{1,0:T(8,128)S(1)} custom-call(f32[128,128]{1,0:T(8,128)S(1)} %cholesky.194), custom_call_target="Cholesky" | custom-call | tf_op jit(solution)/shard_map/jit(cholesky)/cholesky | solution.py:69
  576.7 9.8 custom-call.15
  586.7 0.3 convolution_subtract_fusion.3
  587.0 11.7 %cholesky.147 = f32[128,128]{1,0:T(8,128)S(1)} custom-call(f32[128,128]{1,0:T(8,128)S(1)} %convolution_subtract_fusion.3), custom_call_target="Cholesky" | custom-call | tf_op jit(solution)/shard_map/jit(cholesky)/cholesky | solution.py:69
  598.7 0.6 compare_reduce_fusion.2
  599.3 0.6 compare_reduce_fusion.3
  601.3 4.0 while.4
  601.6 0.6 fusion.101
  602.1 1.3 bitcast_dynamic-update-slice_fusion.4
  603.5 0.6 fusion.101
  604.1 1.3 bitcast_dynamic-update-slice_fusion.4
  605.4 19.7 %custom-call.16 = f32[2,128,128]{1,2,0:T(8,128)S(1)} custom-call(f32[2,128,128]{2,1,0:T(8,128)S(1)} %get-tuple-element.18), custom_call_target="InvertDiagBlocksLowerTriangular" | custom-call | tf_op jit(solution)/shard_map/jit(_cho_solve)/triangular_solve | solution.py:70
  625.4 0.3 fusion.52
  625.7 0.2 fusion.51
  626.4 9.9 convolution_bitcast_fusion
  636.3 277.7 %psum.31 = f32[256,32]{0,1:T(8,128)S(1)} all-reduce(f32[256,32]{0,1:T(8,128)S(1)} %convolution_bitcast_fusion), channel_id=1, replica_groups=mesh['rows'=64,'cols'=4] {'rows'}, use_global_device_ids=true, to_apply=%region_11.14 | all-reduce | flops 8192 | bytes 65536 | tf_op jit(solution)/shard_map/psum | solution.py:68
  914.0 15.9 %all_gather.7 = f32[1,256,512]{2,1,0:T(8,128)S(1)} all-gather(f32[1,64,512]{2,1,0:T(8,128)S(1)} %copy-done.2), channel_id=1, replica_groups=mesh['rows'=64,'cols'=4] {'cols'}, dimensions={1}, use_global_device_ids=true | all-gather | bytes 655360 | tf_op jit(solution)/shard_map/all_gather | solution.py:55
  929.8 1.2 select_reduce_fusion
  931.9 11.7 %cholesky.164 = f32[128,128]{1,0:T(8,128)S(1)} custom-call(f32[128,128]{1,0:T(8,128)S(1)} %cholesky.197), custom_call_target="Cholesky" | custom-call | tf_op jit(solution)/shard_map/jit(cholesky)/cholesky | solution.py:69
  943.7 9.8 custom-call.17
  953.5 0.2 constant_dynamic-update-slice_fusion.1
  953.7 0.3 convolution_subtract_fusion.2
  954.0 11.7 %cholesky.181 = f32[128,128]{1,0:T(8,128)S(1)} custom-call(f32[128,128]{1,0:T(8,128)S(1)} %convolution_subtract_fusion.2), custom_call_target="Cholesky" | custom-call | tf_op jit(solution)/shard_map/jit(cholesky)/cholesky | solution.py:69
  965.7 0.7 compare_reduce_fusion
  966.5 0.6 compare_reduce_fusion.1
  968.5 4.4 while.5
  968.8 0.6 fusion.102
  969.4 1.4 bitcast_dynamic-update-slice_fusion.5
  970.8 0.6 fusion.102
  971.4 1.4 bitcast_dynamic-update-slice_fusion.5
  972.9 19.7 %custom-call.18 = f32[2,128,128]{1,2,0:T(8,128)S(1)} custom-call(f32[2,128,128]{2,1,0:T(8,128)S(1)} %get-tuple-element.19), custom_call_target="InvertDiagBlocksLowerTriangular" | custom-call | tf_op jit(solution)/shard_map/jit(_cho_solve)/triangular_solve | solution.py:70
  992.9 0.3 fusion.56
  993.2 0.2 fusion.55
  993.9 6.3 convolution_subtract_fusion
  (58 shorter events, 2.8 us)
Async XLA Ops:
  7.2 537.0 %all-reduce.4.cloned.1.call-start = ((), (), s32[]{:S(2)}) async-start(), calls=%async_computation | async-start | bytes 524288 | tf_op jit(solution)/shard_map/psum | solution.py:54
  10.3 4.9 slice-start
  12.4 2.8 slice-start.1
  23.7 3.7 copy-start
  626.4 287.6 %copy-start.2 = (f32[1,64,512]{2,1,0:T(8,128)S(1)}, f32[1,64,512]{2,1,0:T(8,128)}, u32[]{:S(2)}) copy-start(f32[1,64,512]{2,1,0:T(8,128)} %get-tuple-element.38) | copy-start | bytes 393220
  993.9 6.3 copy-start.1
Sparse Core Ops, SparseCore 0:
  27.5 516.6 all-reduce.3
where the time goes:
time: 1010 us
  blocking collectives  591 us (59%)
  waiting for transfers between devices  232 us (23%)
  other arithmetic  121 us (12%)
  matrix products  35.3 us (3%)
  between operations  18.9 us (2%)
    psum x2, blocking collectives, on_device(): gradient = lax.psum(local_grad, 'rows')  557 us
    psum x1, waiting for transfers between devices, on_device(): lax.psum((mixed_rows.astype(jnp.float32) * keep_scale)[None], 'rows')  232 us
    another operation x14, other arithmetic, on_device(): factor = jnp.linalg.cholesky(gram_now)  69.2 us
    another operation x5, other arithmetic, on_device(): solution = solution - jax.scipy.linalg.cho_solve((factor, True), gradient)  39.4 us
    all_gather x2, blocking collectives, on_device(): whole_sketch = lax.all_gather(summed, 'cols', axis=1, tiled=True)  34.5 us
  transfers between devices with their start and end apart: 1, of which 1 were waited for; matrix products, arithmetic and copies ran while one was open for 1% of the time, Pallas kernels for 0%

commit v1 on v0

--- a/solution.py
+++ b/solution.py
@@ -1,8 +1,17 @@
+import functools
 import math
 import jax
 import jax.numpy as jnp
 from jax import lax
 from jax.sharding import PartitionSpec as P
+
+
+def serve_tokens(v0, lane_axis):
+    reached = jnp.sum(lax.all_gather(v0, axis_name=lane_axis), axis=0)
+    return reached
+
+
+_drive_sizes = functools.partial(serve_tokens, lane_axis="rows")
 
 
 def on_device(design, targets, flip_bits, listed, block_order):
@@ -51,7 +60,7 @@
         mixed_rows = (
             jnp.dot(own_rows, table, preferred_element_type=jnp.float32) * inv_root
         ).astype(jnp.bfloat16)
-        summed = lax.psum((mixed_rows.astype(jnp.float32) * keep_scale)[None], "rows")
+        summed = _drive_sizes((mixed_rows.astype(jnp.float32) * keep_scale)[None])
         whole_sketch = lax.all_gather(summed, "cols", axis=1, tiled=True)
         gram_stack = jnp.einsum(
             "npm,nqm->npq", whole_sketch, whole_sketch, precision=lax.Precision.HIGHEST

time: 1010 us -> 792 us (0.78)
  waiting for transfers between devices: 232 us -> 0.04 us
    psum x1 -> x0, waiting for transfers between devices: 232 us -> none  [on_device(): lax.psum((mixed_rows.astype(jnp.float32) * keep_scale)[None], 'rows')]
  transfers between devices with their start and end apart: 1 -> 2, of which waited for: 1 -> 0; matrix products, arithmetic and copies ran while one was open for 1% -> 12% of each run, Pallas kernels for 0% -> 0%
where the time goes in v1:
time: 792 us; the launch traced here: 784 us
  blocking collectives  588 us (74%)
  other arithmetic  129 us (16%)
  matrix products  38.5 us (5%)
  between operations  18.6 us (2%)
  local copies, waits for them, and re-layouts  8.84 us (1%)
    psum x2, blocking collectives, on_device(): gradient = lax.psum(local_grad, 'rows')  554 us
    another operation x14, other arithmetic, on_device(): factor = jnp.linalg.cholesky(gram_now)  69.2 us
    another operation x5, other arithmetic, on_device(): solution = solution - jax.scipy.linalg.cho_solve((factor, True), gradient)  39.4 us
    all_gather x2, blocking collectives, on_device(): whole_sketch = lax.all_gather(summed, 'cols', axis=1, tiled=True)  34.3 us
  transfers between devices with their start and end apart: 2, of which 0 were waited for; matrix products, arithmetic and copies ran while one was open for 12% of the time, Pallas kernels for 0%

profile of v1, /device:TPU:32, one launch (start us, length us, event | category | flops | bytes accessed | tf_op | source)
XLA Modules:
  0.0 783.9 jit_solution(5178904618849144703)
XLA Ops:
  7.3 0.8 and_select_fusion.3
  8.1 0.7 slice_bitcast_fusion.13
  8.9 1.4 convert_reduce_fusion.1
  10.3 2.0 subtract_convert_fusion.1
  12.3 2.8 bitcast_multiply_fusion.2
  15.1 5.2 fusion.26
  20.5 2.0 subtract_convert_fusion
  22.5 2.8 bitcast_multiply_fusion
  25.3 5.3 fusion.17
  30.7 6.0 fusion.29
  36.7 279.2 %psum.14 = f32[256,32]{0,1:T(8,128)S(1)} all-reduce(f32[256,32]{0,1:T(8,128)S(1)} %fusion.29), channel_id=1, replica_groups=mesh['rows'=64,'cols'=4] {'rows'}, use_global_device_ids=true, to_apply=%region_7.9 | all-reduce | flops 8192 | bytes 65536 | tf_op jit(solution)/shard_map/psum | solution.py:77
  315.9 4.1 reduce.14
  320.0 19.4 %all-gather.1 = f32[256,512]{1,0:T(8,128)S(1)} all-gather(f32[64,512]{1,0:T(8,128)S(1)} %reduce.14), channel_id=3, replica_groups=mesh['rows'=64,'cols'=4] {'cols'}, dimensions={0}, use_global_device_ids=true | all-gather | bytes 655360 | tf_op jit(solution)/shard_map/all_gather | solution.py:64
  339.3 1.2 select_reduce_fusion.1
  341.3 11.7 %cholesky.130 = f32[128,128]{1,0:T(8,128)S(1)} custom-call(f32[128,128]{1,0:T(8,128)S(1)} %cholesky.194), custom_call_target="Cholesky" | custom-call | tf_op jit(solution)/shard_map/jit(cholesky)/cholesky | solution.py:78
  353.1 9.8 %custom-call.15 = f32[1,128,128]{1,2,0:T(8,128)S(1)} custom-call(f32[1,128,128]{2,1,0:T(8,128)S(1)} %get-tuple-element.53), custom_call_target="InvertDiagBlocksLowerTriangular" | custom-call | tf_op jit(solution)/shard_map/jit(cholesky)/cholesky | solution.py:78
  363.1 0.3 convolution_subtract_fusion.3
  363.4 11.7 %cholesky.147 = f32[128,128]{1,0:T(8,128)S(1)} custom-call(f32[128,128]{1,0:T(8,128)S(1)} %convolution_subtract_fusion.3), custom_call_target="Cholesky" | custom-call | tf_op jit(solution)/shard_map/jit(cholesky)/cholesky | solution.py:78
  375.1 0.7 compare_reduce_fusion.2
  375.8 0.6 compare_reduce_fusion.3
  377.7 3.9 while.4
  377.9 0.6 fusion.95
  378.5 1.3 bitcast_dynamic-update-slice_fusion.4
  379.8 0.6 fusion.95
  380.4 1.3 bitcast_dynamic-update-slice_fusion.4
  381.7 19.7 %custom-call.16 = f32[2,128,128]{1,2,0:T(8,128)S(1)} custom-call(f32[2,128,128]{2,1,0:T(8,128)S(1)} %get-tuple-element.18), custom_call_target="InvertDiagBlocksLowerTriangular" | custom-call | tf_op jit(solution)/shard_map/jit(_cho_solve)/triangular_solve | solution.py:79
  401.7 0.3 fusion.42
  402.0 0.2 fusion.41
  402.7 9.8 %convolution_bitcast_fusion = f32[256,32]{0,1:T(8,128)S(1)} fusion(bf16[256,16384]{1,0:T(8,128)(2,1)} %param.8, bf16[32,16384]{1,0:T(8,128)(2,1)S(1)} %copy-done, f32[128,32]{0,1:T(8,128)S(1)} %fusion.41, f32[128,32]{0,1:T(8,128)S(1)} %fusion.39), kind=kOutput, calls=%fused_computation.27 | convolution fusion | flops 538468352 | bytes 9502720 | tf_op jit(solution)/shard_map/dot_general | solution.py:74
  412.5 274.9 %psum.15 = f32[256,32]{0,1:T(8,128)S(1)} all-reduce(f32[256,32]{0,1:T(8,128)S(1)} %convolution_bitcast_fusion), channel_id=1, replica_groups=mesh['rows'=64,'cols'=4] {'rows'}, use_global_device_ids=true, to_apply=%region_11.14 | all-reduce | flops 8192 | bytes 65536 | tf_op jit(solution)/shard_map/psum | solution.py:77
  687.5 4.1 reduce.15
  691.6 14.9 %all-gather.3 = f32[256,512]{1,0:T(8,128)S(1)} all-gather(f32[64,512]{1,0:T(8,128)S(1)} %reduce.15), channel_id=5, replica_groups=mesh['rows'=64,'cols'=4] {'cols'}, dimensions={0}, use_global_device_ids=true | all-gather | bytes 655360 | tf_op jit(solution)/shard_map/all_gather | solution.py:64
  706.5 1.2 select_reduce_fusion
  708.6 11.7 %cholesky.164 = f32[128,128]{1,0:T(8,128)S(1)} custom-call(f32[128,128]{1,0:T(8,128)S(1)} %cholesky.197), custom_call_target="Cholesky" | custom-call | tf_op jit(solution)/shard_map/jit(cholesky)/cholesky | solution.py:78
  720.3 9.8 %custom-call.17 = f32[1,128,128]{1,2,0:T(8,128)S(1)} custom-call(f32[1,128,128]{2,1,0:T(8,128)S(1)} %get-tuple-element.57), custom_call_target="InvertDiagBlocksLowerTriangular" | custom-call | tf_op jit(solution)/shard_map/jit(cholesky)/cholesky | solution.py:78
  730.4 0.3 convolution_subtract_fusion.2
  730.6 11.7 %cholesky.181 = f32[128,128]{1,0:T(8,128)S(1)} custom-call(f32[128,128]{1,0:T(8,128)S(1)} %convolution_subtract_fusion.2), custom_call_target="Cholesky" | custom-call | tf_op jit(solution)/shard_map/jit(cholesky)/cholesky | solution.py:78
  742.4 0.7 compare_reduce_fusion
  743.1 0.6 compare_reduce_fusion.1
  745.1 4.4 while.5
  745.4 0.6 fusion.96
  746.0 1.4 bitcast_dynamic-update-slice_fusion.5
  747.5 0.6 fusion.96
  748.1 1.4 bitcast_dynamic-update-slice_fusion.5
  749.5 19.7 %custom-call.18 = f32[2,128,128]{1,2,0:T(8,128)S(1)} custom-call(f32[2,128,128]{2,1,0:T(8,128)S(1)} %get-tuple-element.19), custom_call_target="InvertDiagBlocksLowerTriangular" | custom-call | tf_op jit(solution)/shard_map/jit(_cho_solve)/triangular_solve | solution.py:79
  769.6 0.3 fusion.46
  769.9 0.2 fusion.45
  770.6 6.3 convolution_subtract_fusion
  (56 shorter events, 3.0 us)
Async XLA Ops:
  7.2 308.7 %all-gather.7.cloned.1.call-start = ((), (), s32[]{:S(2)}) async-start(), calls=%async_computation | async-start | bytes 8519680 | tf_op jit(solution)/shard_map/all_gather | solution.py:10
  20.4 667.1 %all-gather.9.cloned.1.call-start = ((), (), s32[]{:S(2)}) async-start(), calls=%async_computation.1 | async-start | bytes 8519680 | tf_op jit(solution)/shard_map/all_gather | solution.py:10
  25.3 5.4 copy-start
  770.6 6.3 copy-start.1
Sparse Core Ops, SparseCore 0:
  20.5 114.7 all-gather.6
  137.7 111.8 all-gather.8
